TPU v7x, 32 devices: a whole 2x2x4 slice. The times are simulated.
32 devices in a mesh: dp: 4 (over y, core), fsdp: 4 (over z), tensor: 2 (over x).
Axes of the slice: x: 2, y: 2, z: 4, core: 2. Of those that a mesh axis runs over, the one named last changes fastest.
Arguments:
- hidden_in: bfloat16 [7168, 8192], P(('dp', 'fsdp')), may hold values from -6 to 6
- queries: bfloat16 [7168, 8192], P(('dp', 'fsdp'), 'tensor')
- keys: bfloat16 [7168, 1024], P(('dp', 'fsdp'), 'tensor')
- output_gradient: bfloat16 [7168, 8192], P(('dp', 'fsdp'), 'tensor'), may hold values from -6 to 6
- rewards: float32 [16], P(('dp', 'fsdp')), may hold values from 0 to 4
- lengths: int32 [16], P(('dp', 'fsdp')), may hold values from 112 to 448
- master: float32 [8192, 1024], P(('dp', 'fsdp'), 'tensor'), may hold values from -0.0625 to 0.0625
- moment: float32 [8192, 1024], P(('dp', 'fsdp'), 'tensor'), may hold values from -6 to 6
- adam_second_moment: float32 [8192, 1024], P(('dp', 'fsdp'), 'tensor'), may hold values from 0.25 to 4
- layout: int32 [8], replicated, may hold values from 0 to 7, each once
Outputs:
- updated_master_weight: float32 [8192, 1024], P(('dp', 'fsdp'), 'tensor')
- new_moment: float32 [8192, 1024], P(('dp', 'fsdp'), 'tensor')
- new_second: float32 [8192, 1024], P(('dp', 'fsdp'), 'tensor')
- rollout_value_weight: bfloat16 [8192, 1024], P(('dp', 'fsdp'), 'tensor')
All inputs are finite; a program needn't handle non-finite values.
Results may differ from a plain program's by a relative error of at most 0.0014.
Values may be sent and summed in bfloat16 or wider, within the bound.
A program may use at most 192 MiB of HBM per device.

v0:
```python
import jax
import jax.numpy as jnp
from jax import lax
from jax.sharding import PartitionSpec as P

HEAD_SIZE = 128
QUERY_PER_VALUE = 8


def value_grad(query_matrix, key_matrix, out_rows, value_weight, length):
    token_slot_index = query_matrix.shape[0]
    heads_local = key_matrix.shape[1] // HEAD_SIZE
    query_head_rows = query_matrix.reshape(
        token_slot_index, heads_local, QUERY_PER_VALUE, HEAD_SIZE
    )
    key_head_rows = key_matrix.reshape(token_slot_index, heads_local, HEAD_SIZE)
    scores = jnp.einsum(
        "tkgd,skd->kgts", query_head_rows, key_head_rows, preferred_element_type=jnp.float32
    ) / jnp.sqrt(jnp.float32(HEAD_SIZE))
    position = jnp.arange(token_slot_index)
    allowed = (position[None, :] <= position[:, None]) & (position[None, :] < length)
    scores = jnp.where(allowed[None, None], scores, jnp.float32(-1e30))
    top = jnp.max(scores, axis=-1, keepdims=True)
    expo = jnp.exp(scores - top)
    probs = (expo / jnp.sum(expo, axis=-1, keepdims=True)).astype(jnp.bfloat16)
    attention_gradient = (value_weight[:, None] * out_rows.astype(jnp.float32)).astype(jnp.bfloat16)
    head_gradient = attention_gradient.reshape(
        token_slot_index, heads_local, QUERY_PER_VALUE, HEAD_SIZE
    )
    value_gradient = jnp.einsum(
        "kgts,tkgd->skd", probs, head_gradient, preferred_element_type=jnp.float32
    )
    return value_gradient.reshape(token_slot_index, heads_local * HEAD_SIZE).astype(jnp.bfloat16)


def on_device(
    hidden_in,
    queries,
    keys,
    output_gradient,
    rewards,
    lengths,
    master,
    moment,
    adam_second_moment,
    layout,
):
    reward_sum, length_sum = lax.psum(
        (jnp.sum(rewards), jnp.sum(lengths).astype(jnp.float32)), ("dp", "fsdp")
    )
    seq_count = jnp.float32(lax.axis_size(("dp", "fsdp")))
    advantage = rewards[0] - reward_sum / seq_count
    position = jnp.arange(hidden_in.shape[0])
    value_weight = jnp.where(
        position < lengths[0], advantage * seq_count / length_sum, jnp.float32(0.0)
    )
    value_gradient = value_grad(queries, keys, output_gradient, value_weight, lengths[0])
    grad = lax.psum_scatter(
        lax.dot_general(
            hidden_in, value_gradient, (((0,), (0,)), ((), ())), preferred_element_type=jnp.float32
        ),
        ("dp", "fsdp"),
        scatter_dimension=0,
        tiled=True,
    )
    new_moment = 0.9 * moment + 0.1 * grad
    new_second = 0.95 * adam_second_moment + 0.05 * grad * grad
    corrected = new_moment / (1.0 - 0.9**10) / (jnp.sqrt(new_second / (1.0 - 0.95**10)) + 1e-08)
    updated_master_weight = master - 0.002 * (corrected + 0.1 * master)
    rounded_weight = updated_master_weight.astype(jnp.bfloat16)
    row_count = rounded_weight.shape[0]
    heads_local = rounded_weight.shape[1] // HEAD_SIZE
    targets = lax.dynamic_slice_in_dim(layout, lax.axis_index("tensor") * heads_local, heads_local)
    piece = lax.all_gather(rounded_weight, "tensor", axis=1, tiled=True)
    piece_heads = piece.shape[1] // HEAD_SIZE
    piece_rows = piece.reshape(row_count, piece_heads, HEAD_SIZE)
    carry_rows = jnp.zeros_like(rounded_weight).reshape(row_count, heads_local, HEAD_SIZE)
    chosen = []
    for slot in range(heads_local):
        wanted = targets[slot]
        inside = (wanted >= 0) & (wanted < piece_heads)
        offset = jnp.clip(wanted, 0, piece_heads - 1)
        candidate = lax.dynamic_index_in_dim(piece_rows, offset, 1, keepdims=False)
        chosen.append(jnp.where(inside, candidate, carry_rows[:, slot]))
    rollout_value_weight = jnp.stack(chosen, axis=1).reshape(row_count, heads_local * HEAD_SIZE)
    return (updated_master_weight, new_moment, new_second, rollout_value_weight)


def solution(mesh):
    placed = (
        P(("dp", "fsdp"), None),
        P(("dp", "fsdp"), "tensor"),
        P(("dp", "fsdp"), "tensor"),
        P(("dp", "fsdp"), "tensor"),
        P(("dp", "fsdp")),
        P(("dp", "fsdp")),
        P(("dp", "fsdp"), "tensor"),
        P(("dp", "fsdp"), "tensor"),
        P(("dp", "fsdp"), "tensor"),
        P(),
    )
    return jax.shard_map(
        on_device,
        mesh=mesh,
        in_specs=placed,
        out_specs=(
            P(("dp", "fsdp"), "tensor"),
            P(("dp", "fsdp"), "tensor"),
            P(("dp", "fsdp"), "tensor"),
            P(("dp", "fsdp"), "tensor"),
        ),
        check_vma=False,
    )
```

profile of v0, /device:TPU:0, one launch (start us, length us, event | category | flops | bytes accessed | tf_op | source)
XLA Modules:
  0.0 377.8 jit_solution(9101465570995655895)
XLA Ops:
  7.2 0.0 copy-start.4
  7.2 0.0 reduce-scatter.2.cloned.1.call-start
  8.6 35.8 %all-reduce = (f32[]{:T(128)}, f32[]{:T(128)}) all-reduce(f32[]{:T(128)} %bitcast.1, f32[]{:T(128)S(6)} %convert_element_type.24), channel_id=1, replica_groups=mesh['dp'=4,'fsdp'=4,'tensor'=2] {'dp','fsdp'}, use_global_device_ids=true, to_apply=%region_0.0 | all-reduce | flops 2 | bytes 16 | tf_op jit(solution)/shard_map/psum | solution.py:48
  45.7 0.0 copy-start
  45.7 3.3 fusion.5
  49.1 2.8 copy.44
  51.9 0.1 fusion.11
  52.0 0.0 copy-done
  52.0 2.9 copy.45
  54.9 0.0 copy-done.4
  54.9 0.1 reshape.103
  55.0 16.2 %fusion.6 = f32[4,448,448,8]{2,1,3,0:T(8,128)} fusion(bf16[448,4,8,128]{3,2,1,0:T(8,128)(2,1)} %bitcast.53, bf16[448,4,128,1]{2,1,0,3:T(4,128)(2,1)S(1)} %bitcast.56), kind=kOutput, calls=%fused_computation.11 | convolution fusion | flops 1644167168 | bytes 29818880 | tf_op jit(solution)/shard_map/tkgd,skd->kgts/dot_general | solution.py:17
  71.3 29.3 %fusion.20 = (f32[4,8,448]{2,1,0:T(8,128)S(1)}, f32[4,8,448,448]{2,3,1,0:T(8,128)}) fusion(f32[4,448,448,8]{2,1,3,0:T(8,128)} %fusion.6, pred[448,448]{0,1:T(8,128)(4,1)S(1)} %fusion.11), kind=kOutput, calls=%fused_computation.36 | output fusion | flops 38535616 | bytes 51638272 | tf_op jit(solution)/shard_map/sub | solution.py:24
  100.6 17.7 %divide_convert_fusion = bf16[4,8,448,448]{2,3,1,0:T(8,128)(2,1)} fusion(f32[4,8,448,448]{2,3,1,0:T(8,128)} %get-tuple-element.27, f32[4,8,448]{2,1,0:T(8,128)S(1)} %get-tuple-element.26), kind=kLoop, calls=%fused_computation.2 | loop fusion | flops 12845056 | bytes 38592512 | tf_op jit(solution)/shard_map/convert_element_type | solution.py:25
  118.2 28.1 %copy.39 = bf16[4,8,448,448]{3,1,0,2:T(8,128)(2,1)} copy(bf16[4,8,448,448]{2,3,1,0:T(8,128)(2,1)} %divide_convert_fusion) | data formatting | bytes 25690112 | tf_op jit(solution)/shard_map/convert_element_type | solution.py:25
  146.3 11.0 %fusion.9 = bf16[4,56,8,128]{3,2,1,0:T(8,128)(2,1)S(1)} fusion(bf16[448,4,8,128]{3,2,1,0:T(8,128)(2,1)} %bitcast.52, bf16[4,8,448,448]{3,1,0,2:T(8,128)(2,1)} %copy.39), kind=kOutput, calls=%fused_computation.16 | convolution fusion | flops 1644396544 | bytes 16973824 | tf_op jit(solution)/shard_map/kgts,tkgd->skd/dot_general | solution.py:30
  157.2 11.2 %convolution_bitcast_fusion = f32[8192,512]{0,1:T(8,128)} fusion(bf16[448,8192]{1,0:T(8,128)(2,1)} %param.10, bf16[4,56,8,128]{3,2,1,0:T(8,128)(2,1)S(1)} %fusion.9), kind=kOutput, calls=%fused_computation.8 | convolution fusion | flops 3758096384 | bytes 24576000 | tf_op jit(solution)/shard_map/dot_general | solution.py:59
  168.4 0.0 copy-start.1
  168.4 0.0 copy-start.2
  168.5 0.0 copy-start.3
  168.5 0.0 copy-start.5
  168.5 0.0 reduce-scatter.2.cloned.1.call-update
  168.5 0.0 all-gather.2.cloned.1.call-start
  168.5 1.1 copy-done.1
  169.7 1.3 copy.25
  171.0 0.0 copy-done.2
  171.0 1.3 copy.30
  172.3 0.0 copy-done.3
  172.3 1.3 copy.32
  173.6 170.9 %reduce-scatter.2.cloned.1.call-done = f32[512,512]{0,1:T(8,128)} async-done(((f32[8192,512]{0,1:T(8,128)}), f32[512,512]{0,1:T(8,128)}) %reduce-scatter.2.cloned.1.call-update) | async-done | bytes 1048592 | tf_op jit(solution)/shard_map/reduce_scatter | solution.py:58
  344.5 3.8 %fusion.17 = (bf16[512,512]{0,1:T(8,128)(2,1)}, f32[512,512]{0,1:T(8,128)S(1)}, f32[512,512]{0,1:T(8,128)S(1)}, f32[512,512]{0,1:T(8,128)S(1)}) fusion(f32[512,512]{0,1:T(8,128)} %copy.32, f32[512,512]{0,1:T(8,128)} %reduce-scatter.2.cloned.1.call-done, f32[512,512]{0,1:T(8,128)} %copy.25, f32[512,512]{0,1:T(8,128)} %copy.30), kind=kLoop, calls=%fused_computation.34 | loop fusion | flops 4194304 | bytes 7864320 | tf_op jit(solution)/shard_map/convert_element_type | solution.py:70
  348.3 0.0 all-gather.2.cloned.1.call-update
  348.3 0.0 copy-done.5
  348.3 0.1 dynamic_slice.16
  348.4 0.7 fusion.19
  356.8 1.3 copy.34
  358.1 1.3 copy.35
  359.4 1.3 copy.36
  360.7 8.1 %all-gather.2.cloned.1.call-done = bf16[512,1024]{0,1:T(8,128)(2,1)} async-done(((bf16[512,512]{0,1:T(8,128)(2,1)}), bf16[512,1024]{0,1:T(8,128)(2,1)}) %all-gather.2.cloned.1.call-update) | async-done | bytes 1048592 | tf_op jit(solution)/shard_map/all_gather | solution.py:74
  368.8 1.1 dynamic-slice_select_fusion.3
  369.9 0.1 pad_maximum_fusion
  370.0 1.0 copy.42
  (2 shorter events, 0.0 us)
Async XLA Ops:
  7.2 47.7 %copy-start.4 = (bf16[448,512]{1,0:T(8,128)(2,1)S(1)}, bf16[448,512]{1,0:T(8,128)(2,1)}, u32[]{:S(2)}) copy-start(bf16[448,512]{1,0:T(8,128)(2,1)} %param.12) | copy-start | bytes 1376260
  7.2 337.3 %reduce-scatter.2.cloned.1.call-start = ((), (), s32[]{:S(2)}) async-start(), calls=%async_computation.1 | async-start | bytes 17825792 | tf_op jit(solution)/shard_map/reduce_scatter | solution.py:58
  45.7 6.3 %copy-start = (bf16[448,4096]{1,0:T(8,128)(2,1)S(1)}, bf16[448,4096]{1,0:T(8,128)(2,1)}, u32[]{:S(2)}) copy-start(bf16[448,4096]{1,0:T(8,128)(2,1)} %param.11) | copy-start | bytes 11010052
  168.4 1.2 copy-start.1
  168.4 2.5 copy-start.2
  168.5 3.8 %copy-start.3 = (f32[512,512]{1,0:T(8,128)S(1)}, f32[512,512]{1,0:T(8,128)}, u32[]{:S(2)}) copy-start(f32[512,512]{1,0:T(8,128)} %param.16) | copy-start | bytes 3145732
  168.5 179.9 %copy-start.5 = (s32[8]{0:T(128)S(1)}, s32[8]{0:T(128)}, u32[]{:S(2)}) copy-start(s32[8]{0:T(128)} %param.19) | copy-start | bytes 100
  168.5 200.3 %all-gather.2.cloned.1.call-start = ((), (), s32[]{:S(2)}) async-start(), calls=%async_computation.2 | async-start | bytes 1572864 | tf_op jit(solution)/shard_map/all_gather | solution.py:74
Sparse Core Ops, SparseCore 0:
  168.6 175.8 reduce-scatter.1
  348.4 20.2 all-gather.1
where the time goes:
time: 379 us; the launch traced here: 378 us
  waiting for transfers between devices  179 us (47%)
  other arithmetic  55.4 us (15%)
  local copies, waits for them, and re-layouts  44.6 us (12%)
  matrix products  38.4 us (10%)
  blocking collectives  35.8 us (9%)
  between operations  24.5 us (6%)
    reduce_scatter x1, waiting for transfers between devices, on_device(): lax.psum_scatter(lax.dot_general(hidden_in, value_gradient, (((0,), (0,))...  171 us
    psum x1, blocking collectives, on_device(): lax.psum((jnp.sum(rewards), jnp.sum(lengths).astype(jnp.float32)), ('dp',...  35.8 us
    sub x1, other arithmetic, value_grad(): expo = jnp.exp(scores - top)  29.3 us
    convert_element_type x1, local copies, waits for them, and re-layouts, value_grad(): probs = (expo / jnp.sum(expo, axis=-1, keepdims=True)).astype(jnp.bfloat16)  28.1 us
    convert_element_type x1, other arithmetic, value_grad(): probs = (expo / jnp.sum(expo, axis=-1, keepdims=True)).astype(jnp.bfloat16)  17.7 us
    dot_general x1, matrix products, value_grad(): jnp.einsum('tkgd,skd->kgts', query_head_rows, key_head_rows, preferred_el...  16.2 us
    unnamed x20, local copies, waits for them, and re-layouts  14.7 us
    dot_general x1, matrix products, on_device(): lax.dot_general(hidden_in, value_gradient, (((0,), (0,)), ((), ())), pref...  11.2 us
  transfers between devices with their start and end apart: 2, of which 2 were waited for; matrix products, arithmetic and copies ran while one was open for 2% of the time, Pallas kernels for 0%

commit v1 on v0

--- a/solution.py
+++ b/solution.py
@@ -71,7 +71,15 @@
     row_count = rounded_weight.shape[0]
     heads_local = rounded_weight.shape[1] // HEAD_SIZE
     targets = lax.dynamic_slice_in_dim(layout, lax.axis_index("tensor") * heads_local, heads_local)
-    piece = lax.all_gather(rounded_weight, "tensor", axis=1, tiled=True)
+    ways, here, step = (lax.axis_size("tensor"), lax.axis_index("tensor"), rounded_weight.shape[1])
+    line, have = (rounded_weight, 1)
+    while have < ways:
+        line = jnp.concatenate(
+            [line, lax.ppermute(line, "tensor", [(d, (d - have) % ways) for d in range(ways)])],
+            axis=1,
+        )
+        have = 2 * have
+    piece = jnp.roll(line, here * step, axis=1)
     piece_heads = piece.shape[1] // HEAD_SIZE
     piece_rows = piece.reshape(row_count, piece_heads, HEAD_SIZE)
     carry_rows = jnp.zeros_like(rounded_weight).reshape(row_count, heads_local, HEAD_SIZE)

time: 379 us -> 374 us (0.987)
  waiting for transfers between devices: 179 us -> 171 us
    all_gather x1 -> x0, waiting for transfers between devices: 8.08 us -> none  [on_device(): piece = lax.all_gather(rounded_weight, 'tensor', axis=1, tiled=True)]
    unnamed x20 -> x21, local copies, waits for them, and re-layouts: 14.7 us -> 15.8 us
where the time goes in v1:
time: 374 us; the launch traced here: 373 us
  waiting for transfers between devices  171 us (46%)
  other arithmetic  56.8 us (15%)
  local copies, waits for them, and re-layouts  44.6 us (12%)
  matrix products  38.5 us (10%)
  blocking collectives  35.8 us (10%)
  between operations  24.3 us (6%)
    reduce_scatter x1, waiting for transfers between devices, on_device(): lax.psum_scatter(lax.dot_general(hidden_in, value_gradient, (((0,), (0,))...  171 us
    psum x1, blocking collectives, on_device(): lax.psum((jnp.sum(rewards), jnp.sum(lengths).astype(jnp.float32)), ('dp',...  35.8 us
    sub x1, other arithmetic, value_grad(): expo = jnp.exp(scores - top)  29.3 us
    convert_element_type x1, local copies, waits for them, and re-layouts, value_grad(): probs = (expo / jnp.sum(expo, axis=-1, keepdims=True)).astype(jnp.bfloat16)  28 us
    convert_element_type x1, other arithmetic, value_grad(): probs = (expo / jnp.sum(expo, axis=-1, keepdims=True)).astype(jnp.bfloat16)  17.7 us
    dot_general x1, matrix products, value_grad(): jnp.einsum('tkgd,skd->kgts', query_head_rows, key_head_rows, preferred_el...  16.3 us
    unnamed x21, local copies, waits for them, and re-layouts  15.8 us
    dot_general x1, matrix products, on_device(): lax.dot_general(hidden_in, value_gradient, (((0,), (0,)), ((), ())), pref...  11.2 us
  transfers between devices with their start and end apart: 2, of which 2 were waited for; matrix products, arithmetic and copies ran while one was open for 2% of the time, Pallas kernels for 0%

profile of v1, /device:TPU:0, one launch (start us, length us, event | category | flops | bytes accessed | tf_op | source)
XLA Modules:
  0.0 372.6 jit_solution(15000107305018211756)
XLA Ops:
  7.2 0.0 reduce-scatter.2.cloned.1.call-start
  8.5 35.8 %all-reduce = (f32[]{:T(128)}, f32[]{:T(128)}) all-reduce(f32[]{:T(128)} %bitcast.1, f32[]{:T(128)S(6)} %convert_element_type.24), channel_id=1, replica_groups=mesh['dp'=4,'fsdp'=4,'tensor'=2] {'dp','fsdp'}, use_global_device_ids=true, to_apply=%region_0.0 | all-reduce | flops 2 | bytes 16 | tf_op jit(solution)/shard_map/psum | solution.py:48
  45.7 0.0 copy-start
  45.7 3.3 fusion.5
  49.0 0.0 copy-start.4
  49.0 2.8 copy.42
  51.9 0.1 fusion.14
  52.0 0.0 copy-done
  52.0 2.9 copy.43
  54.9 0.0 copy-done.4
  54.9 0.1 reshape.103
  55.0 16.3 %fusion.6 = f32[4,448,448,8]{2,1,3,0:T(8,128)} fusion(bf16[448,4,8,128]{3,2,1,0:T(8,128)(2,1)} %bitcast.53, bf16[448,4,128,1]{2,1,0,3:T(4,128)(2,1)S(1)} %bitcast.57), kind=kOutput, calls=%fused_computation.11 | convolution fusion | flops 1644167168 | bytes 29818880 | tf_op jit(solution)/shard_map/tkgd,skd->kgts/dot_general | solution.py:17
  71.3 29.3 %fusion.23 = (f32[4,8,448]{2,1,0:T(8,128)S(1)}, f32[4,8,448,448]{2,3,1,0:T(8,128)}) fusion(f32[4,448,448,8]{2,1,3,0:T(8,128)} %fusion.6, pred[448,448]{0,1:T(8,128)(4,1)S(1)} %fusion.14), kind=kOutput, calls=%fused_computation.43 | output fusion | flops 38535616 | bytes 51638272 | tf_op jit(solution)/shard_map/sub | solution.py:24
  100.6 17.7 %divide_convert_fusion = bf16[4,8,448,448]{2,3,1,0:T(8,128)(2,1)} fusion(f32[4,8,448,448]{2,3,1,0:T(8,128)} %get-tuple-element.27, f32[4,8,448]{2,1,0:T(8,128)S(1)} %get-tuple-element.26), kind=kLoop, calls=%fused_computation.2 | loop fusion | flops 12845056 | bytes 38592512 | tf_op jit(solution)/shard_map/convert_element_type | solution.py:25
  118.2 28.0 %copy.38 = bf16[4,8,448,448]{3,1,0,2:T(8,128)(2,1)} copy(bf16[4,8,448,448]{2,3,1,0:T(8,128)(2,1)} %divide_convert_fusion) | data formatting | bytes 25690112 | tf_op jit(solution)/shard_map/convert_element_type | solution.py:25
  146.2 11.0 %fusion.9 = bf16[4,56,8,128]{3,2,1,0:T(8,128)(2,1)S(1)} fusion(bf16[448,4,8,128]{3,2,1,0:T(8,128)(2,1)} %bitcast.52, bf16[4,8,448,448]{3,1,0,2:T(8,128)(2,1)} %copy.38), kind=kOutput, calls=%fused_computation.20 | convolution fusion | flops 1644396544 | bytes 16973824 | tf_op jit(solution)/shard_map/kgts,tkgd->skd/dot_general | solution.py:30
  157.2 11.2 %convolution_bitcast_fusion = f32[8192,512]{0,1:T(8,128)} fusion(bf16[448,8192]{1,0:T(8,128)(2,1)} %param.10, bf16[4,56,8,128]{3,2,1,0:T(8,128)(2,1)S(1)} %fusion.9), kind=kOutput, calls=%fused_computation.8 | convolution fusion | flops 3758096384 | bytes 24576000 | tf_op jit(solution)/shard_map/dot_general | solution.py:59
  168.4 0.0 copy-start.1
  168.4 0.0 copy-start.2
  168.4 0.0 copy-start.3
  168.4 0.0 reduce-scatter.2.cloned.1.call-update
  168.5 1.2 copy-done.1
  169.7 0.0 copy-start.5
  169.7 1.3 copy.24
  171.0 0.0 copy-done.2
  171.0 1.3 copy.29
  172.3 0.0 copy-done.3
  172.3 1.3 copy.31
  173.6 170.7 %reduce-scatter.2.cloned.1.call-done = f32[512,512]{0,1:T(8,128)} async-done(((f32[8192,512]{0,1:T(8,128)}), f32[512,512]{0,1:T(8,128)}) %reduce-scatter.2.cloned.1.call-update) | async-done | bytes 1048592 | tf_op jit(solution)/shard_map/reduce_scatter | solution.py:58
  344.3 3.8 %fusion.20 = (bf16[512,512]{0,1:T(8,128)(2,1)}, f32[512,512]{0,1:T(8,128)S(1)}, f32[512,512]{0,1:T(8,128)S(1)}, f32[512,512]{0,1:T(8,128)S(1)}) fusion(f32[512,512]{0,1:T(8,128)} %copy.31, f32[512,512]{0,1:T(8,128)} %reduce-scatter.2.cloned.1.call-done, f32[512,512]{0,1:T(8,128)} %copy.24, f32[512,512]{0,1:T(8,128)} %copy.29), kind=kLoop, calls=%fused_computation.41 | loop fusion | flops 4194304 | bytes 7864320 | tf_op jit(solution)/shard_map/convert_element_type | solution.py:70
  348.1 1.4 collective-permute-start
  349.6 0.0 copy-done.5
  349.6 0.1 dynamic_slice.20
  349.6 0.6 fusion.22
  357.8 1.3 copy.32
  359.1 1.3 copy.33
  360.4 1.3 copy.34
  361.7 0.5 collective-permute-done
  362.2 2.5 fusion.13
  364.7 0.1 pad_maximum_fusion
  364.8 1.0 copy.35
  (3 shorter events, 0.1 us)
Async XLA Ops:
  7.2 337.2 %reduce-scatter.2.cloned.1.call-start = ((), (), s32[]{:S(2)}) async-start(), calls=%async_computation.1 | async-start | bytes 17825792 | tf_op jit(solution)/shard_map/reduce_scatter | solution.py:58
  45.7 6.3 %copy-start = (bf16[448,4096]{1,0:T(8,128)(2,1)S(1)}, bf16[448,4096]{1,0:T(8,128)(2,1)}, u32[]{:S(2)}) copy-start(bf16[448,4096]{1,0:T(8,128)(2,1)} %param.11) | copy-start | bytes 11010052
  49.0 5.9 %copy-start.4 = (bf16[448,512]{1,0:T(8,128)(2,1)S(1)}, bf16[448,512]{1,0:T(8,128)(2,1)}, u32[]{:S(2)}) copy-start(bf16[448,512]{1,0:T(8,128)(2,1)} %param.12) | copy-start | bytes 1376260
  168.4 1.2 copy-start.1
  168.4 2.5 copy-start.2
  168.4 3.8 %copy-start.3 = (f32[512,512]{1,0:T(8,128)S(1)}, f32[512,512]{1,0:T(8,128)}, u32[]{:S(2)}) copy-start(f32[512,512]{1,0:T(8,128)} %param.16) | copy-start | bytes 3145732
  169.7 179.9 %copy-start.5 = (s32[8]{0:T(128)S(1)}, s32[8]{0:T(128)}, u32[]{:S(2)}) copy-start(s32[8]{0:T(128)} %param.19) | copy-start | bytes 100
  348.1 14.0 %collective-permute-start = (bf16[512,512]{0,1:T(8,128)(2,1)}, bf16[512,512]{0,1:T(8,128)(2,1)}, u32[]{:S(2)}, u32[]{:S(2)}) collective-permute-start(bf16[512,512]{0,1:T(8,128)(2,1)} %get-tuple-element.14), channel_id=1, source_target_pairs={{0,1},{1,0},{2,3},{3,2},{4,5},{5,4},{6,7},{7,6},{8,9},{9,8},{10,11... | collective-permute-start | bytes 1572872 | tf_op jit(solution)/shard_map/ppermute | solution.py:78
Sparse Core Ops, SparseCore 0:
  168.6 175.6 reduce-scatter.1
